TPU v7x, 32 devices: a whole 2x2x4 slice. The times are simulated.
32 devices in a mesh: mem: 8 (over z, core), slab: 4 (over y, x).
Axes of the slice: x: 2, y: 2, z: 4, core: 2. Of those that a mesh axis runs over, the one named last changes fastest.
Arguments:
- thickness: float32 [64, 256, 384], P('mem', 'slab'), may hold values from 0.5 to 2.5
- face_u: float32 [256, 384], P('slab'), may hold values from -0.4 to 0.4
- face_v: float32 [256, 384], P('slab'), may hold values from -0.4 to 0.4
- obs_cells: int32 [512, 4], P('slab'), may hold values from 0 to 98303, as said below
- obs_weights: int32 [512, 4], P('slab'), may hold values from 1 to 4
- obs_values: float32 [512], P('slab'), may hold values from -6 to 6
- obs_noise: float32 [64, 512], P('mem', 'slab'), may hold values from -3 to 3
- cov_inverse: float32 [512, 512], P('slab'), may hold values from -0.375 to 0.375
- taper_mask: int32 [4, 4], replicated, may hold values from 0 to 1, as said below
Outputs:
- analysis: float32 [64, 256, 384], P('mem', 'slab')
Inputs may be any that keep to these rules, and one draw needn't show every extreme that they name: `obs_cells`: observation o covers a 2 x 2 square of cells, all within the rows of slab o // 128. `taper_mask`: entries are 0 or 1 and the diagonal is 1.
All inputs are finite; a program needn't handle non-finite values.
Results may differ from a plain program's by a relative error of at most 0.0003.
Values sent between devices are 32-bit elements; how exact they have to be, the bound alone decides.
A program may use at most 64 MiB of HBM per device.

v0:
```python
import jax
import jax.numpy as jnp
from jax import lax
from jax.sharding import PartitionSpec as P


def padded_2(block, sides, width):
    for axis, dim in sides:
        count = lax.axis_size(axis)
        forward = [(i, i + 1) for i in range(count - 1)]
        backward = [(target, source) for source, target in forward]
        low = lax.ppermute(
            lax.slice_in_dim(block, block.shape[dim] - width, None, axis=dim), axis, forward
        )
        high = lax.ppermute(lax.slice_in_dim(block, 0, width, axis=dim), axis, backward)
        block = jnp.concatenate([low, block, high], axis=dim)
    return block


def minmod(first_diff, second_diff):
    return (
        0.5
        * (jnp.sign(first_diff) + jnp.sign(second_diff))
        * jnp.minimum(jnp.abs(first_diff), jnp.abs(second_diff))
    )


def face_flux(padded, velocity, axis_dim):
    counted = padded.shape[axis_dim] - 3
    far_low = lax.slice_in_dim(padded, 0, counted, axis=axis_dim)
    near_low = lax.slice_in_dim(padded, 1, 1 + counted, axis=axis_dim)
    near_high = lax.slice_in_dim(padded, 2, 2 + counted, axis=axis_dim)
    far_high = lax.slice_in_dim(padded, 3, 3 + counted, axis=axis_dim)
    left_state = near_low + 0.5 * minmod(near_low - far_low, near_high - near_low)
    right_state = near_high - 0.5 * minmod(near_high - near_low, far_high - near_high)
    return jnp.maximum(velocity, 0.0) * left_state + jnp.minimum(velocity, 0.0) * right_state


def local(
    thickness,
    face_u,
    face_v,
    obs_cells,
    obs_weights,
    obs_values,
    obs_noise,
    cov_inverse,
    taper_mask,
):
    member_subset = thickness.shape[0]
    band_rows = thickness.shape[1]
    column_list = thickness.shape[2]
    slab_index = lax.axis_index("slab")
    stacked = jnp.concatenate([thickness, face_v[None]], 0)
    padded = padded_2(stacked, (("slab", 1),), 2)
    row_pad = padded[:member_subset]
    row_speed = padded[member_subset, 2 : band_rows + 3]
    row_fluxes = face_flux(row_pad, row_speed, 1)
    col_pad = jnp.pad(thickness, ((0, 0), (0, 0), (2, 2)))
    col_speed = jnp.pad(face_u, ((0, 0), (0, 1)))
    column_fluxes = face_flux(col_pad, col_speed, 2)
    prior_state = (
        thickness
        - (column_fluxes[:, :, 1:] - column_fluxes[:, :, :-1])
        - (row_fluxes[:, 1:, :] - row_fluxes[:, :-1, :])
    )
    state_vector = prior_state.reshape(member_subset, band_rows * column_list)
    local_cells = obs_cells - slab_index * (band_rows * column_list)
    weights = obs_weights.astype(jnp.float32)
    picked = state_vector[:, local_cells]
    obs_model = jnp.sum(picked * weights[None], -1) / jnp.sum(weights, -1)[None]
    innovation = obs_values[None, :] + obs_noise - obs_model
    white_terms = jnp.dot(innovation, cov_inverse, precision=lax.Precision.HIGHEST)
    whitened = lax.psum_scatter(white_terms, "slab", scatter_dimension=1, tiled=True)
    model_all, white_all = (
        lax.all_gather(obs_model, "mem", axis=0, tiled=True),
        lax.all_gather(whitened, "mem", axis=0, tiled=True),
    )
    obs_mean = jnp.mean(model_all, 0, keepdims=True)
    cell_state = lax.all_to_all(state_vector, "mem", split_axis=1, concat_axis=0, tiled=True)
    members = cell_state.shape[0]
    anomaly = cell_state - jnp.mean(cell_state, 0, keepdims=True)
    obs_anomaly = model_all - obs_mean
    anom_full, white_full = (
        lax.all_gather(obs_anomaly, "slab", axis=1, tiled=True),
        lax.all_gather(white_all, "slab", axis=1, tiled=True),
    )
    block_size = obs_anomaly.shape[1]
    mask_row = lax.dynamic_slice_in_dim(taper_mask, slab_index, 1, 0)[0].astype(jnp.float32)
    taper_row = jnp.repeat(mask_row, block_size)
    cross = lax.dot_general(
        anomaly, anom_full, (((0,), (0,)), ((), ())), precision=lax.Precision.HIGHEST
    ) / (members - 1)
    tapered = cross * taper_row[None, :]
    update = lax.dot_general(
        white_full, tapered, (((1,), (1,)), ((), ())), precision=lax.Precision.HIGHEST
    )
    analysis_cells = cell_state + update
    returned = lax.all_to_all(analysis_cells, "mem", split_axis=0, concat_axis=1, tiled=True)
    return returned.reshape(member_subset, band_rows, column_list)


def solution(mesh):
    return jax.shard_map(
        local,
        mesh=mesh,
        in_specs=(
            P("mem", "slab", None),
            P("slab", None),
            P("slab", None),
            P("slab", None),
            P("slab", None),
            P("slab"),
            P("mem", "slab"),
            P("slab", None),
            P(),
        ),
        out_specs=P("mem", "slab", None),
        check_vma=False,
    )
```

profile of v0, /device:TPU:0, one launch (start us, length us, event | category | flops | bytes accessed | tf_op | source)
XLA Modules:
  0.0 138.8 jit_solution(13175700690734752969)
XLA Ops:
  6.5 0.0 copy-start
  6.5 0.0 copy-start.1
  6.5 1.1 pad_maximum_fusion.3
  7.6 1.3 collective-permute-start
  8.9 5.5 %collective-permute-start.1 = (f32[9,2,384]{2,1,0:T(2,128)S(1)}, f32[9,2,384]{2,1,0:T(2,128)S(1)}, u32[]{:S(2)}, u32[]{:S(2)}) collective-permute-start(f32[9,2,384]{2,1,0:T(2,128)S(1)} %get-tuple-element.9), channel_id=1, source_target_pairs={{0,1},{1,2},{2,3},{4,5},{5,6},{6,7},{8,9},{9,10},{10,11},{12,13},{... | collective-permute-start | bytes 82952 | tf_op jit(solution)/shard_map/ppermute | solution.py:12
  14.4 0.9 pad_maximum_fusion.1
  15.4 0.7 compare_select_fusion
  16.1 0.1 copy.36
  16.2 0.1 reshape.37
  16.3 3.6 %multiply_add_fusion = f32[8,64,385]{2,1,0:T(8,128)S(1)} fusion(f32[8,64,384]{2,1,0:T(8,128)} %param.9, f32[64,385]{1,0:T(8,128)S(1)} %get-tuple-element.12, f32[64,385]{1,0:T(8,128)S(1)} %get-tuple-element.11), kind=kLoop, calls=%fused_computation.12 | loop fusion | flops 4730880 | bytes 1772032 | tf_op jit(solution)/shard_map/add | solution.py:36
  19.9 0.7 convert_reduce_fusion
  20.6 0.0 collective-permute-done
  20.6 0.9 maximum_bitcast_fusion
  21.6 0.0 collective-permute-done.1
  21.6 1.6 %maximum_maximum_fusion = (f32[9,66,384]{2,1,0:T(8,128)S(1)}, f32[9,66,384]{2,1,0:T(8,128)S(1)}) fusion(f32[1,64,384]{2,1,0:T(8,128)} %bitcast.30, f32[8,64,384]{2,1,0:T(8,128)} %param.9, f32[9,2,384]{2,1,0:T(2,128)S(1)} %collective-permute-done.1, f32[9,2,384]{2,1,0:T(2,128)S(1)} %collective-permute-done), kind=kLoop, calls=%fused_computation.14 | loop fusion | flops 912384 | bytes 2764800 | tf_op jit(solution)/shard_map/concatenate | solution.py:16
  23.2 0.0 copy-start.2
  23.2 1.3 multiply_add_fusion.1
  24.5 0.0 copy-done.1
  24.5 0.3 fusion.11
  24.9 0.1 all_to_all.26
  25.0 1.3 copy.34
  26.4 5.4 %all-to-all-start = ((f32[8,8,3072]{2,0,1:T(8,128)}), f32[8,8,3072]{2,0,1:T(8,128)S(1)}, u32[]{:S(2)}, u32[]{:S(2)}) async-start(f32[8,8,3072]{2,0,1:T(8,128)} %copy.34), calls=%async_computation | async-start | bytes 1572864 | tf_op jit(solution)/shard_map/all_to_all | solution.py:80
  31.8 0.0 reduce-scatter.2.cloned.1.call-start
  31.8 0.7 multiply_bitcast_fusion
  32.5 0.0 copy-done.2
  32.5 0.1 copy.37
  32.6 0.1 broadcast_bitcast_fusion
  32.7 0.0 copy-start.3
  32.7 6.6 %copy.35 = f32[8,64,384]{0,2,1:T(8,128)} copy(f32[8,64,384]{2,1,0:T(8,128)S(1)} %fusion.11) | data formatting | bytes 1572864 | tf_op jit(solution)/shard_map/sub | solution.py:63
  39.2 5.6 %gather_fusion = f32[512,8]{1,0:T(8,128)S(1)} fusion(f32[8,24576]{0,1:T(8,128)} %bitcast.25, s32[1024]{0:T(1024)S(1)} %pad_clamp_fusion), kind=kCustom, calls=%fused_computation | custom fusion | bytes 34816 | tf_op jit(solution)/shard_map/gather | solution.py:70
  44.9 0.2 multiply_reduce_fusion
  45.2 0.0 copy-done
  45.2 0.0 copy-done.3
  45.2 0.0 copy-done.4
  45.2 0.8 fusion.15
  46.0 0.0 reduce-scatter.2.cloned.1.call-update
  46.1 14.6 %all_gather.14 = f32[64,128]{1,0:T(8,128)S(1)} all-gather(f32[8,128]{1,0:T(8,128)S(1)} %divide_bitcast_fusion), channel_id=1, replica_groups=mesh['mem'=8,'slab'=4] {'mem'}, dimensions={0}, use_global_device_ids=true | all-gather | bytes 36864 | tf_op jit(solution)/shard_map/all_gather | solution.py:76
  60.7 9.9 %all_gather.15 = f32[64,512]{1,0:T(8,128)S(1)} all-gather(f32[64,128]{1,0:T(8,128)S(1)} %broadcast_subtract_fusion), channel_id=1, replica_groups=mesh['mem'=8,'slab'=4] {'slab'}, dimensions={1}, use_global_device_ids=true | all-gather | bytes 163840 | tf_op jit(solution)/shard_map/all_gather | solution.py:85
  70.6 0.0 reduce-scatter.2.cloned.1.call-done
  70.6 14.2 %all_gather.12 = f32[64,128]{1,0:T(8,128)S(1)} all-gather(f32[8,128]{1,0:T(8,128)} %reduce-scatter.2.cloned.1.call-done), channel_id=1, replica_groups=mesh['mem'=8,'slab'=4] {'mem'}, dimensions={0}, use_global_device_ids=true | all-gather | bytes 36864 | tf_op jit(solution)/shard_map/all_gather | solution.py:77
  84.7 9.0 %all_gather.13 = f32[64,512]{1,0:T(8,128)S(1)} all-gather(f32[64,128]{1,0:T(8,128)S(1)} %all_gather.12), channel_id=1, replica_groups=mesh['mem'=8,'slab'=4] {'slab'}, dimensions={1}, use_global_device_ids=true | all-gather | bytes 163840 | tf_op jit(solution)/shard_map/all_gather | solution.py:86
  93.8 0.0 all-to-all-done
  93.8 0.1 reduce_sum.38
  93.8 5.2 %fusion.13 = f32[3072,512]{1,0:T(8,128)S(1)} fusion(f32[64,512]{1,0:T(8,128)S(1)} %all_gather.15, f32[8,8,3072]{2,0,1:T(8,128)S(1)} %all-to-all-done, f32[3072]{0:T(1024)S(1)} %broadcast_multiply_fusion), kind=kOutput, calls=%fused_computation.23 | convolution fusion | flops 1208156160 | bytes 7221248 | tf_op jit(solution)/shard_map/dot_general | solution.py:91
  99.0 6.0 %fusion.5 = f32[8,8,3072]{2,1,0:T(8,128)S(1)} fusion(f32[64,512]{1,0:T(8,128)S(1)} %all_gather.13, f32[3072,512]{1,0:T(8,128)S(1)} %fusion.13, f32[512]{0:T(512)S(1)} %broadcast_bitcast_fusion, f32[8,8,3072]{2,0,1:T(8,128)S(1)} %all-to-all-done), kind=kOutput, calls=%fused_computation.4 | convolution fusion | flops 1209729024 | bytes 7997440 | tf_op jit(solution)/shard_map/dot_general | solution.py:95
  105.1 25.4 %all_to_all.35 = f32[8,8,3072]{2,1,0:T(8,128)S(1)} all-to-all(f32[8,8,3072]{2,1,0:T(8,128)S(1)} %fusion.5), channel_id=1, replica_groups=mesh['mem'=8,'slab'=4] {'mem'}, dimensions={0} | all-to-all | bytes 1572864 | tf_op jit(solution)/shard_map/all_to_all | solution.py:99
  130.5 0.5 copy.39
  130.9 1.0 reshape.34
  (10 shorter events, 0.1 us)
Async XLA Ops:
  6.5 38.6 %copy-start = (f32[128,512]{1,0:T(8,128)S(1)}, f32[128,512]{1,0:T(8,128)}, u32[]{:S(2)}) copy-start(f32[128,512]{1,0:T(8,128)} %param.16) | copy-start | bytes 786436
  6.5 18.0 %copy-start.1 = (f32[8,64,384]{2,1,0:T(8,128)S(1)}, f32[8,64,384]{2,1,0:T(8,128)}, u32[]{:S(2)}) copy-start(f32[8,64,384]{2,1,0:T(8,128)} %param.9) | copy-start | bytes 2359300
  7.6 13.0 %collective-permute-start = (f32[9,2,384]{2,1,0:T(2,128)S(1)}, f32[9,2,384]{2,1,0:T(2,128)S(1)}, u32[]{:S(2)}, u32[]{:S(2)}) collective-permute-start(f32[9,2,384]{2,1,0:T(2,128)S(1)} %get-tuple-element.10), channel_id=1, source_target_pairs={{1,0},{2,1},{3,2},{5,4},{6,5},{7,6},{9,8},{10,9},{11,10},{13,12},{... | collective-permute-start | bytes 82952 | tf_op jit(solution)/shard_map/ppermute | solution.py:15
  8.9 12.6 %collective-permute-start.1 = (f32[9,2,384]{2,1,0:T(2,128)S(1)}, f32[9,2,384]{2,1,0:T(2,128)S(1)}, u32[]{:S(2)}, u32[]{:S(2)}) collective-permute-start(f32[9,2,384]{2,1,0:T(2,128)S(1)} %get-tuple-element.9), channel_id=1, source_target_pairs={{0,1},{1,2},{2,3},{4,5},{5,6},{6,7},{8,9},{9,10},{10,11},{12,13},{... | collective-permute-start | bytes 82952 | tf_op jit(solution)/shard_map/ppermute | solution.py:12
  23.2 9.3 %copy-start.2 = (s32[128,4]{0,1:T(4,128)S(1)}, s32[128,4]{0,1:T(4,128)}, u32[]{:S(2)}) copy-start(s32[128,4]{0,1:T(4,128)} %param.13) | copy-start | bytes 6148
  26.4 67.4 %all-to-all-start = ((f32[8,8,3072]{2,0,1:T(8,128)}), f32[8,8,3072]{2,0,1:T(8,128)S(1)}, u32[]{:S(2)}, u32[]{:S(2)}) async-start(f32[8,8,3072]{2,0,1:T(8,128)} %copy.34), calls=%async_computation | async-start | bytes 1572864 | tf_op jit(solution)/shard_map/all_to_all | solution.py:80
  31.8 38.8 %reduce-scatter.2.cloned.1.call-start = ((), (), s32[]{:S(2)}) async-start(), calls=%async_computation.3 | async-start | bytes 20480 | tf_op jit(solution)/shard_map/reduce_scatter | solution.py:74
  32.7 12.5 %copy-start.3 = (f32[8,128]{1,0:T(8,128)S(1)}, f32[8,128]{1,0:T(8,128)}, u32[]{:S(2)}) copy-start(f32[8,128]{1,0:T(8,128)} %param.15) | copy-start | bytes 12292
  32.7 12.5 %copy-start.4 = (f32[128]{0:T(128)S(1)}, f32[128]{0:T(128)}, u32[]{:S(2)}) copy-start(f32[128]{0:T(128)} %param.14) | copy-start | bytes 1540
Sparse Core Ops, SparseCore 0:
  46.2 24.1 reduce-scatter.1
where the time goes:
time: 139 us
  blocking collectives  73 us (53%)
  local copies, waits for them, and re-layouts  15.6 us (11%)
  between operations  13.6 us (10%)
  other arithmetic  12.3 us (9%)
  starting transfers between devices  12.2 us (9%)
  matrix products  12.1 us (9%)
    all_to_all x1, blocking collectives, local(): lax.all_to_all(analysis_cells, 'mem', split_axis=0, concat_axis=1, tiled=...  25.4 us
    all_gather x1, blocking collectives, local(): lax.all_gather(obs_model, 'mem', axis=0, tiled=True)  14.6 us
    all_gather x1, blocking collectives, local(): lax.all_gather(whitened, 'mem', axis=0, tiled=True)  14.2 us
    all_gather x1, blocking collectives, local(): lax.all_gather(obs_anomaly, 'slab', axis=1, tiled=True)  9.86 us
    all_gather x1, blocking collectives, local(): lax.all_gather(white_all, 'slab', axis=1, tiled=True)  9 us
    sub x1, local copies, waits for them, and re-layouts, local(): thickness - (column_fluxes[:, :, 1:] - column_fluxes[:, :, :-1])  6.56 us
    dot_general x1, matrix products, local(): lax.dot_general(white_full, tapered, (((1,), (1,)), ((), ())), precision=...  6.04 us
    gather x1, local copies, waits for them, and re-layouts, local(): picked = state_vector[:, local_cells]  5.6 us
  transfers between devices with their start and end apart: 4, of which 0 were waited for; matrix products, arithmetic and copies ran while one was open for 15% of the time, Pallas kernels for 0%

commit v1 on v0

--- a/solution.py
+++ b/solution.py
@@ -2,6 +2,43 @@
 import jax.numpy as jnp
 from jax import lax
 from jax.sharding import PartitionSpec as P
+from jax.lax import axis_index, axis_size, ppermute
+
+
+def name_paths_all(z, row_dim, payload):
+    local_out = z.shape
+    shaped = z.reshape(
+        *local_out[:row_dim], payload, local_out[row_dim] // payload, *local_out[row_dim + 1 :]
+    )
+    return jnp.moveaxis(shaped, row_dim, 0)
+
+
+def drive_the_seats_all(in_array, on_dim):
+    in_array = jnp.moveaxis(in_array, 0, on_dim)
+    earlier = in_array.shape
+    return in_array.reshape(
+        *earlier[:on_dim], earlier[on_dim] * earlier[on_dim + 1], *earlier[on_dim + 2 :]
+    )
+
+
+def fix_the_bars(slab_in, lane_axis, block_in, obj):
+    tile_out = axis_size(lane_axis)
+    later = axis_index(lane_axis)
+    right_arr, block_now = (tile_out, later)
+    step_out = name_paths_all(slab_in, block_in, right_arr)
+    column = [step_out[block_now]]
+    for h in range(1, right_arr):
+        state_now = step_out[(block_now + h) % right_arr]
+        column.append(
+            ppermute(
+                state_now,
+                axis_name=lane_axis,
+                perm=[(k, (k + h) % right_arr) for k in range(right_arr)],
+            )
+        )
+    u_next = jnp.stack(column)
+    step_out = u_next[(block_now - jnp.arange(right_arr)) % right_arr]
+    return drive_the_seats_all(step_out, obj)
 
 
 def padded_2(block, sides, width):
@@ -96,7 +133,7 @@
         white_full, tapered, (((1,), (1,)), ((), ())), precision=lax.Precision.HIGHEST
     )
     analysis_cells = cell_state + update
-    returned = lax.all_to_all(analysis_cells, "mem", split_axis=0, concat_axis=1, tiled=True)
+    returned = fix_the_bars(analysis_cells, "mem", 0, 1)
     return returned.reshape(member_subset, band_rows, column_list)
 
 

time: 139 us -> 134 us (0.964)
  the two profiles are of different devices: /device:TPU:0 before, /device:TPU:9 now
where the time goes in v1:
time: 134 us
  blocking collectives  44.6 us (33%)
  starting transfers between devices  20.6 us (15%)
  local copies, waits for them, and re-layouts  16.3 us (12%)
  waiting for transfers between devices  13.9 us (10%)
  between operations  13.8 us (10%)
  other arithmetic  12.3 us (9%)
  matrix products  12.1 us (9%)
    all_gather x1, blocking collectives, local(): lax.all_gather(whitened, 'mem', axis=0, tiled=True)  15.4 us
    all_gather x1, blocking collectives, local(): lax.all_gather(obs_model, 'mem', axis=0, tiled=True)  14.3 us
    ppermute x7, waiting for transfers between devices, fix_the_bars(): ppermute(state_now, axis_name=lane_axis, perm=[(k, (k + h) % right_arr) f...  13 us
    ppermute x7, starting transfers between devices, fix_the_bars(): ppermute(state_now, axis_name=lane_axis, perm=[(k, (k + h) % right_arr) f...  9.17 us
    all_gather x1, blocking collectives, local(): lax.all_gather(obs_anomaly, 'slab', axis=1, tiled=True)  7.85 us
    all_gather x1, blocking collectives, local(): lax.all_gather(white_all, 'slab', axis=1, tiled=True)  7.06 us
    sub x1, local copies, waits for them, and re-layouts, local(): thickness - (column_fluxes[:, :, 1:] - column_fluxes[:, :, :-1])  6.59 us
    all_to_all x1, starting transfers between devices, local(): lax.all_to_all(state_vector, 'mem', split_axis=1, concat_axis=0, tiled=True)  6.16 us
  transfers between devices with their start and end apart: 11, of which 5 were waited for; matrix products, arithmetic and copies ran while one was open for 16% of the time, Pallas kernels for 0%

profile of v1, /device:TPU:9, one launch (start us, length us, event | category | flops | bytes accessed | tf_op | source)
XLA Modules:
  0.0 133.6 jit_solution(4389033448942409546)
XLA Ops:
  6.5 1.1 pad_maximum_fusion.3
  7.6 1.3 collective-permute-start
  8.9 4.0 %collective-permute-start.1 = (f32[9,2,384]{2,1,0:T(2,128)S(1)}, f32[9,2,384]{2,1,0:T(2,128)S(1)}, u32[]{:S(2)}, u32[]{:S(2)}) collective-permute-start(f32[9,2,384]{2,1,0:T(2,128)S(1)} %get-tuple-element.9), channel_id=1, source_target_pairs={{0,1},{1,2},{2,3},{4,5},{5,6},{6,7},{8,9},{9,10},{10,11},{12,13},{... | collective-permute-start | bytes 82952 | tf_op jit(solution)/shard_map/ppermute | solution.py:49
  12.9 0.9 pad_maximum_fusion.1
  13.9 0.7 compare_select_fusion
  14.5 0.1 copy.36
  14.7 0.1 reshape.82
  14.8 0.7 convert_reduce_fusion
  15.5 3.6 %multiply_add_fusion = f32[8,64,385]{2,1,0:T(8,128)S(1)} fusion(f32[8,64,384]{2,1,0:T(8,128)} %param.9, f32[64,385]{1,0:T(8,128)S(1)} %get-tuple-element.20, f32[64,385]{1,0:T(8,128)S(1)} %get-tuple-element.19), kind=kLoop, calls=%fused_computation.13 | loop fusion | flops 4730880 | bytes 1772032 | tf_op jit(solution)/shard_map/add | solution.py:73
  19.1 0.9 maximum_bitcast_fusion
  20.1 1.6 %maximum_maximum_fusion = (f32[9,66,384]{2,1,0:T(8,128)S(1)}, f32[9,66,384]{2,1,0:T(8,128)S(1)}) fusion(f32[1,64,384]{2,1,0:T(8,128)} %bitcast.60, f32[8,64,384]{2,1,0:T(8,128)} %param.9, f32[9,2,384]{2,1,0:T(2,128)S(1)} %collective-permute-done.1, f32[9,2,384]{2,1,0:T(2,128)S(1)} %collective-permute-done), kind=kLoop, calls=%fused_computation.15 | loop fusion | flops 912384 | bytes 2764800 | tf_op jit(solution)/shard_map/concatenate | solution.py:53
  21.7 1.3 multiply_add_fusion.1
  23.1 0.3 fusion.11
  23.4 0.1 all_to_all.14
  23.5 1.3 %copy.34 = f32[8,8,3072]{2,0,1:T(8,128)} copy(f32[8,8,3072]{2,1,0:T(8,128)S(1)} %all_to_all.14) | data formatting | bytes 1572864 | tf_op jit(solution)/shard_map/all_to_all | solution.py:117
  24.9 6.2 %all-to-all-start = ((f32[8,8,3072]{2,0,1:T(8,128)}), f32[8,8,3072]{2,0,1:T(8,128)S(1)}, u32[]{:S(2)}, u32[]{:S(2)}) async-start(f32[8,8,3072]{2,0,1:T(8,128)} %copy.34), calls=%async_computation | async-start | bytes 1572864 | tf_op jit(solution)/shard_map/all_to_all | solution.py:117
  31.0 0.7 fusion.22
  31.8 0.1 copy.37
  32.0 0.1 broadcast_bitcast_fusion
  32.0 6.6 %copy.35 = f32[8,64,384]{0,2,1:T(8,128)} copy(f32[8,64,384]{2,1,0:T(8,128)S(1)} %fusion.11) | data formatting | bytes 1572864 | tf_op jit(solution)/shard_map/sub | solution.py:100
  38.6 5.6 %gather_fusion = f32[512,8]{1,0:T(8,128)S(1)} fusion(f32[8,24576]{0,1:T(8,128)} %bitcast.55, s32[1024]{0:T(1024)S(1)} %pad_clamp_fusion.1), kind=kCustom, calls=%fused_computation | custom fusion | bytes 34816 | tf_op jit(solution)/shard_map/gather | solution.py:107
  44.2 0.2 multiply_reduce_fusion
  44.6 0.0 copy-done.3
  44.6 0.8 fusion.15
  45.4 0.0 reduce-scatter.2.cloned.1.call-update
  45.5 14.3 %all_gather.14 = f32[64,128]{1,0:T(8,128)S(1)} all-gather(f32[8,128]{1,0:T(8,128)S(1)} %divide_bitcast_fusion), channel_id=1, replica_groups=mesh['mem'=8,'slab'=4] {'mem'}, dimensions={0}, use_global_device_ids=true | all-gather | bytes 36864 | tf_op jit(solution)/shard_map/all_gather | solution.py:113
  59.8 7.9 %all_gather.15 = f32[64,512]{1,0:T(8,128)S(1)} all-gather(f32[64,128]{1,0:T(8,128)S(1)} %broadcast_subtract_fusion), channel_id=1, replica_groups=mesh['mem'=8,'slab'=4] {'slab'}, dimensions={1}, use_global_device_ids=true | all-gather | bytes 163840 | tf_op jit(solution)/shard_map/all_gather | solution.py:122
  67.6 0.9 reduce-scatter.2.cloned.1.call-done
  68.5 15.4 %all_gather.12 = f32[64,128]{1,0:T(8,128)S(1)} all-gather(f32[8,128]{1,0:T(8,128)} %reduce-scatter.2.cloned.1.call-done), channel_id=1, replica_groups=mesh['mem'=8,'slab'=4] {'mem'}, dimensions={0}, use_global_device_ids=true | all-gather | bytes 36864 | tf_op jit(solution)/shard_map/all_gather | solution.py:114
  83.9 7.1 %all_gather.13 = f32[64,512]{1,0:T(8,128)S(1)} all-gather(f32[64,128]{1,0:T(8,128)S(1)} %all_gather.12), channel_id=1, replica_groups=mesh['mem'=8,'slab'=4] {'slab'}, dimensions={1}, use_global_device_ids=true | all-gather | bytes 163840 | tf_op jit(solution)/shard_map/all_gather | solution.py:123
  91.0 0.1 reduce_sum.38
  91.0 5.2 %fusion.13 = f32[3072,512]{1,0:T(8,128)S(1)} fusion(f32[64,512]{1,0:T(8,128)S(1)} %all_gather.15, f32[8,8,3072]{2,0,1:T(8,128)S(1)} %all-to-all-done, f32[3072]{0:T(1024)S(1)} %broadcast_multiply_fusion), kind=kOutput, calls=%fused_computation.24 | convolution fusion | flops 1208156160 | bytes 7221248 | tf_op jit(solution)/shard_map/dot_general | solution.py:128
  96.2 6.0 %fusion.5 = f32[8,8,3072]{2,1,0:T(8,128)S(1)} fusion(f32[64,512]{1,0:T(8,128)S(1)} %all_gather.13, f32[3072,512]{1,0:T(8,128)S(1)} %fusion.13, f32[512]{0:T(512)S(1)} %broadcast_bitcast_fusion, f32[8,8,3072]{2,0,1:T(8,128)S(1)} %all-to-all-done), kind=kOutput, calls=%fused_computation.5 | convolution fusion | flops 1209729024 | bytes 7997440 | tf_op jit(solution)/shard_map/dot_general | solution.py:132
  102.3 0.1 dynamic-slice_bitcast_fusion
  102.3 1.5 %collective-permute-start.2 = (f32[8,3072]{1,0:T(8,128)S(1)}, f32[8,3072]{1,0:T(8,128)S(1)}, u32[]{:S(2)}, u32[]{:S(2)}) collective-permute-start(f32[8,3072]{1,0:T(8,128)S(1)} %get-tuple-element.17), channel_id=1, source_target_pairs={{0,4},{4,8},{8,12},{12,16},{16,20},{20,24},{24,28},{28,0},{1,5},{5... | collective-permute-start | bytes 294920 | tf_op jit(solution)/shard_map/ppermute | solution.py:33
  103.9 3.0 %collective-permute-start.3 = (f32[8,3072]{1,0:T(8,128)S(1)}, f32[8,3072]{1,0:T(8,128)S(1)}, u32[]{:S(2)}, u32[]{:S(2)}) collective-permute-start(f32[8,3072]{1,0:T(8,128)S(1)} %get-tuple-element.16), channel_id=1, source_target_pairs={{0,8},{4,12},{8,16},{12,20},{16,24},{20,28},{24,0},{28,4},{1,9},{5... | collective-permute-start | bytes 294920 | tf_op jit(solution)/shard_map/ppermute | solution.py:33
  106.9 0.3 collective-permute-start.4
  107.2 0.8 collective-permute-start.5
  108.0 2.0 %collective-permute-start.6 = (f32[8,3072]{1,0:T(8,128)S(1)}, f32[8,3072]{1,0:T(8,128)S(1)}, u32[]{:S(2)}, u32[]{:S(2)}) collective-permute-start(f32[8,3072]{1,0:T(8,128)S(1)} %get-tuple-element.13), channel_id=1, source_target_pairs={{0,20},{4,24},{8,28},{12,0},{16,4},{20,8},{24,12},{28,16},{1,21},{... | collective-permute-start | bytes 294920 | tf_op jit(solution)/shard_map/ppermute | solution.py:33
  110.1 1.2 collective-permute-start.7
  111.3 0.3 collective-permute-start.8
  111.6 0.7 collective-permute-done.4
  112.2 9.0 %collective-permute-done.5 = f32[8,3072]{1,0:T(8,128)S(1)} collective-permute-done((f32[8,3072]{1,0:T(8,128)S(1)}, f32[8,3072]{1,0:T(8,128)S(1)}, u32[]{:S(2)}, u32[]{:S(2)}) %collective-permute-start.5) | collective-permute-done | bytes 98336 | tf_op jit(solution)/shard_map/ppermute | solution.py:33
  121.3 3.3 %collective-permute-done.7 = f32[8,3072]{1,0:T(8,128)S(1)} collective-permute-done((f32[8,3072]{1,0:T(8,128)S(1)}, f32[8,3072]{1,0:T(8,128)S(1)}, u32[]{:S(2)}, u32[]{:S(2)}) %collective-permute-start.7) | collective-permute-done | bytes 98336 | tf_op jit(solution)/shard_map/ppermute | solution.py:33
  124.6 0.1 collective-permute-done.8
  124.7 0.6 gather_fusion.1
  125.3 0.5 copy.39
  125.7 1.0 reshape_reshape.3
  (34 shorter events, 0.2 us)
Async XLA Ops:
  6.5 38.0 %copy-start = (f32[128,512]{1,0:T(8,128)S(1)}, f32[128,512]{1,0:T(8,128)}, u32[]{:S(2)}) copy-start(f32[128,512]{1,0:T(8,128)} %param.16) | copy-start | bytes 786436
  6.5 16.5 %copy-start.1 = (f32[8,64,384]{2,1,0:T(8,128)S(1)}, f32[8,64,384]{2,1,0:T(8,128)}, u32[]{:S(2)}) copy-start(f32[8,64,384]{2,1,0:T(8,128)} %param.9) | copy-start | bytes 2359300
  7.6 11.5 %collective-permute-start = (f32[9,2,384]{2,1,0:T(2,128)S(1)}, f32[9,2,384]{2,1,0:T(2,128)S(1)}, u32[]{:S(2)}, u32[]{:S(2)}) collective-permute-start(f32[9,2,384]{2,1,0:T(2,128)S(1)} %get-tuple-element.10), channel_id=1, source_target_pairs={{1,0},{2,1},{3,2},{5,4},{6,5},{7,6},{9,8},{10,9},{11,10},{13,12},{... | collective-permute-start | bytes 82952 | tf_op jit(solution)/shard_map/ppermute | solution.py:52
  8.9 11.2 %collective-permute-start.1 = (f32[9,2,384]{2,1,0:T(2,128)S(1)}, f32[9,2,384]{2,1,0:T(2,128)S(1)}, u32[]{:S(2)}, u32[]{:S(2)}) collective-permute-start(f32[9,2,384]{2,1,0:T(2,128)S(1)} %get-tuple-element.9), channel_id=1, source_target_pairs={{0,1},{1,2},{2,3},{4,5},{5,6},{6,7},{8,9},{9,10},{10,11},{12,13},{... | collective-permute-start | bytes 82952 | tf_op jit(solution)/shard_map/ppermute | solution.py:49
  21.7 10.0 %copy-start.2 = (s32[128,4]{0,1:T(4,128)S(1)}, s32[128,4]{0,1:T(4,128)}, u32[]{:S(2)}) copy-start(s32[128,4]{0,1:T(4,128)} %param.13) | copy-start | bytes 6148
  24.9 66.1 %all-to-all-start = ((f32[8,8,3072]{2,0,1:T(8,128)}), f32[8,8,3072]{2,0,1:T(8,128)S(1)}, u32[]{:S(2)}, u32[]{:S(2)}) async-start(f32[8,8,3072]{2,0,1:T(8,128)} %copy.34), calls=%async_computation | async-start | bytes 1572864 | tf_op jit(solution)/shard_map/all_to_all | solution.py:117
  31.0 37.5 %reduce-scatter.2.cloned.1.call-start = ((), (), s32[]{:S(2)}) async-start(), calls=%async_computation.2 | async-start | bytes 20480 | tf_op jit(solution)/shard_map/reduce_scatter | solution.py:111
  32.0 12.5 %copy-start.3 = (f32[8,128]{1,0:T(8,128)S(1)}, f32[8,128]{1,0:T(8,128)}, u32[]{:S(2)}) copy-start(f32[8,128]{1,0:T(8,128)} %param.15) | copy-start | bytes 12292
  32.0 12.5 %copy-start.4 = (f32[128]{0:T(128)S(1)}, f32[128]{0:T(128)}, u32[]{:S(2)}) copy-start(f32[128]{0:T(128)} %param.14) | copy-start | bytes 1540
  102.3 7.7 %collective-permute-start.2 = (f32[8,3072]{1,0:T(8,128)S(1)}, f32[8,3072]{1,0:T(8,128)S(1)}, u32[]{:S(2)}, u32[]{:S(2)}) collective-permute-start(f32[8,3072]{1,0:T(8,128)S(1)} %get-tuple-element.17), channel_id=1, source_target_pairs={{0,4},{4,8},{8,12},{12,16},{16,20},{20,24},{24,28},{28,0},{1,5},{5... | collective-permute-start | bytes 294920 | tf_op jit(solution)/shard_map/ppermute | solution.py:33
  103.9 7.4 %collective-permute-start.3 = (f32[8,3072]{1,0:T(8,128)S(1)}, f32[8,3072]{1,0:T(8,128)S(1)}, u32[]{:S(2)}, u32[]{:S(2)}) collective-permute-start(f32[8,3072]{1,0:T(8,128)S(1)} %get-tuple-element.16), channel_id=1, source_target_pairs={{0,8},{4,12},{8,16},{12,20},{16,24},{20,28},{24,0},{28,4},{1,9},{5... | collective-permute-start | bytes 294920 | tf_op jit(solution)/shard_map/ppermute | solution.py:33
  106.9 5.4 %collective-permute-start.4 = (f32[8,3072]{1,0:T(8,128)S(1)}, f32[8,3072]{1,0:T(8,128)S(1)}, u32[]{:S(2)}, u32[]{:S(2)}) collective-permute-start(f32[8,3072]{1,0:T(8,128)S(1)} %get-tuple-element.15), channel_id=1, source_target_pairs={{0,12},{4,16},{8,20},{12,24},{16,28},{20,0},{24,4},{28,8},{1,13},{... | collective-permute-start | bytes 294920 | tf_op jit(solution)/shard_map/ppermute | solution.py:33
  107.2 14.1 %collective-permute-start.5 = (f32[8,3072]{1,0:T(8,128)S(1)}, f32[8,3072]{1,0:T(8,128)S(1)}, u32[]{:S(2)}, u32[]{:S(2)}) collective-permute-start(f32[8,3072]{1,0:T(8,128)S(1)} %get-tuple-element.14), channel_id=1, source_target_pairs={{0,16},{4,20},{8,24},{12,28},{16,0},{20,4},{24,8},{28,12},{1,17},{... | collective-permute-start | bytes 294920 | tf_op jit(solution)/shard_map/ppermute | solution.py:33
  108.0 13.2 %collective-permute-start.6 = (f32[8,3072]{1,0:T(8,128)S(1)}, f32[8,3072]{1,0:T(8,128)S(1)}, u32[]{:S(2)}, u32[]{:S(2)}) collective-permute-start(f32[8,3072]{1,0:T(8,128)S(1)} %get-tuple-element.13), channel_id=1, source_target_pairs={{0,20},{4,24},{8,28},{12,0},{16,4},{20,8},{24,12},{28,16},{1,21},{... | collective-permute-start | bytes 294920 | tf_op jit(solution)/shard_map/ppermute | solution.py:33
  110.1 14.5 %collective-permute-start.7 = (f32[8,3072]{1,0:T(8,128)S(1)}, f32[8,3072]{1,0:T(8,128)S(1)}, u32[]{:S(2)}, u32[]{:S(2)}) collective-permute-start(f32[8,3072]{1,0:T(8,128)S(1)} %get-tuple-element.12), channel_id=1, source_target_pairs={{0,24},{4,28},{8,0},{12,4},{16,8},{20,12},{24,16},{28,20},{1,25},{... | collective-permute-start | bytes 294920 | tf_op jit(solution)/shard_map/ppermute | solution.py:33
  111.3 13.4 %collective-permute-start.8 = (f32[8,3072]{1,0:T(8,128)S(1)}, f32[8,3072]{1,0:T(8,128)S(1)}, u32[]{:S(2)}, u32[]{:S(2)}) collective-permute-start(f32[8,3072]{1,0:T(8,128)S(1)} %get-tuple-element.11), channel_id=1, source_target_pairs={{0,28},{4,0},{8,4},{12,8},{16,12},{20,16},{24,20},{28,24},{1,29},{... | collective-permute-start | bytes 294920 | tf_op jit(solution)/shard_map/ppermute | solution.py:33
Sparse Core Ops, SparseCore 0:
  45.6 22.9 reduce-scatter.1
